TPU v7x, 32 devices: a whole 2x2x4 slice. The times are simulated.
32 devices in a mesh: seq: 8 (over z, x), head: 4 (over y, core).
Axes of the slice: x: 2, y: 2, z: 4, core: 2. Of those that a mesh axis runs over, the one named last changes fastest.
Arguments:
- tokens: bfloat16 [1024, 2048], P('seq', 'head'), may hold values from -6 to 6
- norm_gain: float32 [2048], replicated, may hold values from 0.1 to 1.9
- query_weight: bfloat16 [2048, 2048], P(None, 'head')
- key_weight: bfloat16 [2048, 256], replicated, may hold values from -0.125 to 0.125
- value_weight: bfloat16 [2048, 256], replicated, may hold values from -0.125 to 0.125
- window_lengths: int32 [8], replicated, may hold values from 1 to 256, 1024 in all
- is_caption: int32 [1024], P('seq'), may hold values 0 or 1
- span_blocks: int32 [8, 2], P('seq'), may hold values from 0 to 7, as said below
Outputs:
- attended: bfloat16 [1024, 2048], P('seq', 'head')
Inputs may be any that keep to these rules, and one draw needn't show every extreme that they name: `window_lengths`: window lengths are whole numbers summing to 1024, the largest exactly 256. `is_caption`: 1 marks a caption token, 0 a visual token. `span_blocks`: row b holds first and last key block of one event span: first <= last <= first + 1 and first <= 6; some span has exactly 2 blocks.
All inputs are finite; a program needn't handle non-finite values. No bound on the sum of `is_caption` on one device may be relied on, other than what follows from the above.
Results may differ from a plain program's by a relative error of at most 0.019.
The roundings to bfloat16 on the way count: a program that leaves them out, or rounds other values in their place, can miss the bound.
Values may be sent and summed in bfloat16 or wider, within the bound.
No kernel may reach another device: no remote copies, remote signals or barrier semaphores. Data moves between devices by JAX's collectives and lax.ppermute only.
A program may use at most 64 MiB of HBM per device.

v0:
```python
import jax
import jax.numpy as jnp
from jax import lax
from jax.sharding import PartitionSpec as P

H = 16
KV = 2
HD = 128
BLOCK = 128
norm_eps = 1e-05
rope_base = 500000.0
window_cap = 4096
span_cap = 8
slice_blocks = 8
lowest_start = -1e30


def rotate(vectors, position):
    half_size = vectors.shape[-1] // 2
    frequency = rope_base ** (-jnp.arange(half_size, dtype=jnp.float32) * 2.0 / vectors.shape[-1])
    angles = position.astype(jnp.float32)[:, None] * frequency[None, :]
    cosine = jnp.cos(angles)[:, None, :]
    sine_part = jnp.sin(angles)[:, None, :]
    first_half = vectors[..., :half_size]
    second_half = vectors[..., half_size:]
    return jnp.concatenate(
        [
            first_half * cosine - second_half * sine_part,
            second_half * cosine + first_half * sine_part,
        ],
        -1,
    )


def rms_normed(tokens, norm_gain):
    hidden = tokens.astype(jnp.float32)
    scale = lax.rsqrt(jnp.mean(hidden * hidden, -1, keepdims=True) + norm_eps)
    return (hidden * scale * norm_gain[None, :]).astype(jnp.bfloat16)


def window_starts(window_lengths, position):
    window_ends = jnp.cumsum(window_lengths)
    begins = window_ends - window_lengths
    within = (begins[None, :] <= position[:, None]) & (position[:, None] < window_ends[None, :])
    return jnp.sum(jnp.where(within, begins[None, :], 0), 1)


def inside(first_row, row_pos, key_pos):
    return (first_row[:, None] <= key_pos[None, :]) & (key_pos[None, :] <= row_pos[:, None])


def absorb(softmax_state, queries, key_values, allowed):
    highest, denominator, weighted = softmax_state
    head_size = queries.shape[-1]
    scores = jnp.einsum(
        "rhd,nd->rhn", queries, key_values[:, :head_size], preferred_element_type=jnp.float32
    )
    scores = jnp.where(allowed[:, None, :], scores, -jnp.inf)
    updated = jnp.maximum(highest, jnp.max(scores, -1))
    rescale = jnp.exp(highest - updated)
    weights = jnp.exp(scores - updated[..., None])
    denominator = rescale * denominator + jnp.sum(weights, -1)
    weighted = rescale[..., None] * weighted + jnp.einsum(
        "rhn,nd->rhd",
        weights.astype(jnp.bfloat16),
        key_values[:, head_size:],
        preferred_element_type=jnp.float32,
    )
    return (updated, denominator, weighted)


def absorb_sliced(softmax_state, queries, key_values, allowed):
    key_count = key_values.shape[0]
    piece = slice_blocks * BLOCK
    for begin in range(0, key_count, piece):
        finish = min(begin + piece, key_count)
        softmax_state = absorb(
            softmax_state, queries, key_values[begin:finish], allowed[:, begin:finish]
        )
    return softmax_state


def select(layout, wanted, total_blocks):
    blocks_dev = layout.shape[0]
    clipped = jnp.clip(wanted, 0, total_blocks - 1)
    return layout[clipped % blocks_dev, clipped // blocks_dev]


def per_device(
    tokens,
    norm_gain,
    query_weight,
    key_weight,
    value_weight,
    window_lengths,
    is_caption,
    span_blocks,
):
    ranks = lax.axis_size("seq")
    device_rank = lax.axis_index("seq")
    features = lax.all_gather(tokens, "head", axis=1, tiled=True)
    local_rows = features.shape[0]
    blocks_dev = local_rows // BLOCK
    total_blocks = blocks_dev * ranks
    window = min(window_cap, total_blocks * BLOCK // 4)
    span_most = min(span_cap, total_blocks // 4)
    window_back = (window + BLOCK - 2) // BLOCK
    first_pos = device_rank * local_rows
    row_pos = first_pos + jnp.arange(local_rows, dtype=jnp.int32)
    normed = rms_normed(features, norm_gain)
    head_dev = query_weight.shape[1] // HD
    kv_index = lax.axis_index("head") * head_dev // (H // KV)
    queries = jnp.dot(normed, query_weight, preferred_element_type=jnp.float32).reshape(
        local_rows, head_dev, HD
    )
    queries = (rotate(queries, row_pos) * HD ** (-0.5)).astype(jnp.bfloat16)
    key_columns = lax.dynamic_slice_in_dim(key_weight, kv_index * HD, HD, 1)
    value_columns = lax.dynamic_slice_in_dim(value_weight, kv_index * HD, HD, 1)
    key_rows = jnp.dot(normed, key_columns, preferred_element_type=jnp.float32).reshape(
        local_rows, 1, HD
    )
    key_rows = rotate(key_rows, row_pos).reshape(local_rows, HD).astype(jnp.bfloat16)
    value_rows = jnp.dot(normed, value_columns, preferred_element_type=jnp.float32).astype(
        jnp.bfloat16
    )
    key_values = jnp.concatenate([key_rows, value_rows], 1)
    window_first = window_starts(window_lengths, row_pos)
    caption_rows = is_caption == 1
    row_block = jnp.arange(local_rows, dtype=jnp.int32) // BLOCK
    span_end = span_blocks[:, 1][row_block]
    all_spans = lax.all_gather(span_blocks, "seq", axis=0, tiled=True)
    pieces = key_values.reshape(blocks_dev, ranks, BLOCK // ranks, 2 * HD)
    layout = lax.all_to_all(pieces, "seq", split_axis=1, concat_axis=1, tiled=True)
    offsets = jnp.arange(span_most, dtype=jnp.int32)
    span_wanted = all_spans[:, 0].reshape(ranks, blocks_dev, 1) + offsets[None, None, :]
    span_wanted = span_wanted.reshape(ranks, blocks_dev * span_most).T
    own_starts = span_blocks[:, 0]
    span_pos = (
        (own_starts[:, None] + offsets[None, :])[:, :, None] * BLOCK
        + jnp.arange(BLOCK, dtype=jnp.int32)[None, None, :]
    ).reshape(-1)
    span_owner = jnp.arange(blocks_dev * span_most * BLOCK, dtype=jnp.int32) // (span_most * BLOCK)
    span_ok = (span_owner[None, :] == row_block[:, None]) & (
        span_pos[None, :] // BLOCK <= span_end[:, None]
    )
    span_ok = span_ok & caption_rows[:, None] & ~inside(window_first, row_pos, span_pos)
    start_state = (
        jnp.full((local_rows, head_dev), lowest_start, jnp.float32),
        jnp.zeros((local_rows, head_dev), jnp.float32),
        jnp.zeros((local_rows, head_dev, HD), jnp.float32),
    )
    near_index = jnp.arange(window_back + blocks_dev, dtype=jnp.int32)
    near_wanted = (
        (jnp.arange(ranks, dtype=jnp.int32) * blocks_dev)[None, :]
        - window_back
        + near_index[:, None]
    )
    wanted = jnp.concatenate([near_wanted, span_wanted], 0)
    delivered = lax.all_to_all(
        select(layout, wanted, total_blocks), "seq", split_axis=1, concat_axis=1, tiled=True
    )
    gathered = delivered.reshape(-1, 2 * HD)
    near_pos = (first_pos // BLOCK - window_back) * BLOCK + jnp.arange(
        (window_back + blocks_dev) * BLOCK, dtype=jnp.int32
    )
    allowed = jnp.concatenate([inside(window_first, row_pos, near_pos), span_ok], 1)
    softmax_state = absorb_sliced(start_state, queries, gathered, allowed)
    highest, denominator, weighted = softmax_state
    return (
        (weighted / denominator[..., None]).reshape(local_rows, head_dev * HD).astype(jnp.bfloat16)
    )


def solution(mesh):
    in_specs = (P("seq", "head"), P(), P(None, "head"), P(), P(), P(), P("seq"), P("seq", None))
    out_specs = P("seq", "head")
    return jax.shard_map(
        per_device, mesh=mesh, in_specs=in_specs, out_specs=out_specs, check_vma=False
    )
```

profile of v0, /device:TPU:0, one launch (start us, length us, event | category | flops | bytes accessed | tf_op | source)
XLA Modules:
  0.0 59.4 jit_solution(15557514870400121325)
XLA Ops:
  0.0 0.0 copy-start
  0.0 0.0 copy-start.1
  0.1 9.0 %all_gather.6 = bf16[128,2048]{1,0:T(8,128)(2,1)S(1)} all-gather(bf16[128,512]{1,0:T(8,128)(2,1)} %param.8), channel_id=1, replica_groups=mesh['seq'=8,'head'=4] {'head'}, dimensions={1}, use_global_device_ids=true | all-gather | bytes 655360 | tf_op jit(solution)/shard_map/all_gather | solution.py:101
  9.1 0.2 fusion.4
  9.3 0.0 copy-start.3
  9.3 0.0 copy-start.4
  9.3 0.0 copy-start.2
  9.3 1.5 %convolution_convert_fusion = bf16[128,128]{0,1:T(8,128)(2,1)S(1)} fusion(bf16[2048,256]{1,0:T(8,128)(2,1)} %param.12, s32[]{:T(128)S(6)} %select_n.76, bf16[128,2048]{1,0:T(8,128)(2,1)S(1)} %all_gather.6, f32[2048]{0:T(1024)} %param.9, f32[128]{0:T(128)S(1)} %add_rsqrt_fusion), kind=kOutput, calls=%fused_computation.11 | convolution fusion | flops 68173824 | bytes 1090052 | tf_op jit(solution)/shard_map/dot_general | solution.py:123
  10.8 0.0 copy-done.1
  10.8 1.5 %convolution_bitcast_fusion = f32[128,1,128]{0,2,1:T(8,128)S(1)} fusion(bf16[2048,256]{1,0:T(8,128)(2,1)} %param.11, s32[]{:T(128)S(6)} %select_n.76, bf16[128,2048]{1,0:T(8,128)(2,1)S(1)} %all_gather.6, f32[2048]{0:T(1024)S(1)} %copy-done.1, f32[128]{0:T(128)S(1)} %add_rsqrt_fusion), kind=kOutput, calls=%fused_computation.10 | convolution fusion | flops 68157440 | bytes 1122820 | tf_op jit(solution)/shard_map/dot_general | solution.py:119
  12.3 0.2 fusion.19
  12.5 0.7 %copy.33 = bf16[128,256]{1,0:T(8,128)(2,1)} copy(bf16[128,256]{0,1:T(8,128)(2,1)S(1)} %pad_maximum_fusion) | data formatting | bytes 131072 | tf_op jit(solution)/shard_map/concatenate | solution.py:126
  13.2 5.8 %all-to-all-start = ((bf16[1,8,16,256]{3,2,0,1:T(8,128)(2,1)}), bf16[1,8,16,256]{3,2,0,1:T(8,128)(2,1)S(1)}, u32[]{:S(2)}, u32[]{:S(2)}) async-start(bf16[1,8,16,256]{3,2,0,1:T(8,128)(2,1)} %bitcast.9), calls=%async_computation | async-start | bytes 131072 | tf_op jit(solution)/shard_map/all_to_all | solution.py:133
  19.1 0.3 multiply_cosine_fusion
  19.4 0.0 copy-done.3
  19.4 0.2 reduce-window.8
  19.6 0.0 copy-done.4
  19.6 0.0 copy-done.2
  19.6 0.6 %fusion.36 = (s32[1,1]{1,0:T(1,128)}, s32[1,1]{1,0:T(1,128)}) fusion(s32[1,2]{1,0:T(1,128)S(1)} %copy-done.2), kind=kLoop, calls=%fused_computation.82 | loop fusion | bytes 16 | tf_op jit(solution)/shard_map/slice | solution.py:130
  20.2 0.6 %add_multiply_fusion = s32[2]{0:T(128)S(1)} fusion(s32[]{:T(128)} %bitcast.2), kind=kLoop, calls=%fused_computation.70 | loop fusion | flops 4 | bytes 12 | tf_op jit(solution)/shard_map/mul | solution.py:139
  20.8 0.1 add.213
  20.9 0.6 %fusion.24 = pred[256]{0:T(512)(128)(4,1)S(1)} fusion(s32[]{:T(128)} %bitcast.5, s32[256]{0:T(256)S(1)} %bitcast.47), kind=kLoop, calls=%fused_computation.65 | loop fusion | flops 4352 | bytes 1284 | tf_op jit(solution)/shard_map/le | solution.py:144
  21.6 21.0 %all-gather = s32[8,1,2]{2,1,0:T(1,128)S(1)} all-gather(s32[1,1,2]{2,1,0:T(1,128)S(1)} %bitcast.45), channel_id=1, replica_groups=mesh['seq'=8,'head'=4] {'seq'}, dimensions={0}, use_global_device_ids=true | all-gather | bytes 72 | tf_op jit(solution)/shard_map/all_gather | solution.py:131
  42.5 0.1 copy.35
  42.7 0.1 reshape.403
  42.7 0.0 copy-done
  42.7 0.5 fusion.33
  43.2 0.1 reshape.399
  43.3 0.1 select_reduce_fusion
  43.4 0.1 compare_and_fusion
  43.6 0.1 not_and_fusion
  43.7 0.0 all-to-all-done
  43.7 0.6 %gather_fusion = bf16[40,16,256]{2,1,0:T(8,128)(2,1)S(1)} fusion(bf16[1,8,16,256]{3,2,1,0:T(8,128)(2,1)S(1)} %bitcast.40, s32[40]{0:T(128)S(1)} %reshape.403), kind=kCustom, calls=%fused_computation | custom fusion | bytes 655680 | tf_op jit(solution)/shard_map/gather | solution.py:86
  44.3 0.7 %copy.37 = bf16[5,8,16,256]{3,2,0,1:T(8,128)(2,1)} copy(bf16[5,8,16,256]{3,2,1,0:T(8,128)(2,1)S(1)} %bitcast.41) | data formatting | bytes 655360 | tf_op jit(solution)/shard_map/gather | solution.py:86
  45.1 3.4 %all-to-all-start.1 = ((bf16[5,8,16,256]{3,2,0,1:T(8,128)(2,1)}), bf16[5,8,16,256]{3,2,0,1:T(8,128)(2,1)S(1)}, u32[]{:S(2)}, u32[]{:S(2)}) async-start(bf16[5,8,16,256]{3,2,0,1:T(8,128)(2,1)} %copy.37), calls=%async_computation.1 | async-start | bytes 655360 | tf_op jit(solution)/shard_map/all_to_all | solution.py:159
  48.6 0.2 fusion.35
  48.8 0.1 multiply_subtract_fusion
  48.8 8.3 %all-to-all-done.1 = bf16[5,8,16,256]{3,2,0,1:T(8,128)(2,1)S(1)} async-done(((bf16[5,8,16,256]{3,2,0,1:T(8,128)(2,1)}), bf16[5,8,16,256]{3,2,0,1:T(8,128)(2,1)S(1)}, u32[]{:S(2)}, u32[]{:S(2)}) %all-to-all-start.1) | async-done | bytes 327712 | tf_op jit(solution)/shard_map/all_to_all | solution.py:159
  57.2 0.5 fusion.37
  57.7 0.4 fusion.1
  58.1 0.5 fusion.3
  58.6 0.8 %copy.40 = bf16[128,512]{1,0:T(8,128)(2,1)} copy(bf16[128,512]{0,1:T(8,128)(2,1)S(1)} %bitcast.44) | data formatting | bytes 262144 | tf_op jit(solution)/shard_map/convert_element_type | solution.py:170
  (19 shorter events, 0.2 us)
Async XLA Ops:
  0.0 42.7 %copy-start = (bf16[2048,512]{1,0:T(8,128)(2,1)S(1)}, bf16[2048,512]{1,0:T(8,128)(2,1)}, u32[]{:S(2)}) copy-start(bf16[2048,512]{1,0:T(8,128)(2,1)} %param.10) | copy-start | bytes 6291460
  0.0 10.8 %copy-start.1 = (f32[2048]{0:T(1024)S(1)}, f32[2048]{0:T(1024)}, u32[]{:S(2)}) copy-start(f32[2048]{0:T(1024)} %param.9) | copy-start | bytes 24580
  9.3 10.1 %copy-start.3 = (s32[8]{0:T(128)S(1)}, s32[8]{0:T(128)}, u32[]{:S(2)}) copy-start(s32[8]{0:T(128)} %param.13) | copy-start | bytes 100
  9.3 10.3 %copy-start.4 = (s32[128]{0:T(128)S(1)}, s32[128]{0:T(128)}, u32[]{:S(2)}) copy-start(s32[128]{0:T(128)} %param.14) | copy-start | bytes 1540
  9.3 10.3 %copy-start.2 = (s32[1,2]{1,0:T(1,128)S(1)}, s32[1,2]{1,0:T(1,128)}, u32[]{:S(2)}) copy-start(s32[1,2]{1,0:T(1,128)} %param.15) | copy-start | bytes 28
  13.2 30.5 %all-to-all-start = ((bf16[1,8,16,256]{3,2,0,1:T(8,128)(2,1)}), bf16[1,8,16,256]{3,2,0,1:T(8,128)(2,1)S(1)}, u32[]{:S(2)}, u32[]{:S(2)}) async-start(bf16[1,8,16,256]{3,2,0,1:T(8,128)(2,1)} %bitcast.9), calls=%async_computation | async-start | bytes 131072 | tf_op jit(solution)/shard_map/all_to_all | solution.py:133
  45.1 12.0 %all-to-all-start.1 = ((bf16[5,8,16,256]{3,2,0,1:T(8,128)(2,1)}), bf16[5,8,16,256]{3,2,0,1:T(8,128)(2,1)S(1)}, u32[]{:S(2)}, u32[]{:S(2)}) async-start(bf16[5,8,16,256]{3,2,0,1:T(8,128)(2,1)} %copy.37), calls=%async_computation.1 | async-start | bytes 655360 | tf_op jit(solution)/shard_map/all_to_all | solution.py:159
where the time goes:
time: 59.8 us; the launch traced here: 59.4 us
  blocking collectives  30 us (50%)
  starting transfers between devices  9.23 us (15%)
  waiting for transfers between devices  8.3 us (14%)
  matrix products  4.45 us (7%)
  local copies, waits for them, and re-layouts  4.08 us (7%)
  other arithmetic  3.04 us (5%)
    all_gather x1, blocking collectives, per_device(): all_spans = lax.all_gather(span_blocks, 'seq', axis=0, tiled=True)  21 us
    all_gather x1, blocking collectives, per_device(): features = lax.all_gather(tokens, 'head', axis=1, tiled=True)  9.02 us
    all_to_all x1, waiting for transfers between devices, per_device(): lax.all_to_all(select(layout, wanted, total_blocks), 'seq', split_axis=1,...  8.3 us
    all_to_all x1, starting transfers between devices, per_device(): lax.all_to_all(pieces, 'seq', split_axis=1, concat_axis=1, tiled=True)  5.8 us
    all_to_all x1, starting transfers between devices, per_device(): lax.all_to_all(select(layout, wanted, total_blocks), 'seq', split_axis=1,...  3.43 us
    dot_general x1, matrix products, per_device(): jnp.dot(normed, value_columns, preferred_element_type=jnp.float32)  1.48 us
    dot_general x1, matrix products, per_device(): jnp.dot(normed, key_columns, preferred_element_type=jnp.float32)  1.45 us
    gather x2, local copies, waits for them, and re-layouts, select(): return layout[clipped % blocks_dev, clipped // blocks_dev]  1.37 us
  transfers between devices with their start and end apart: 2, of which 1 were waited for; matrix products, arithmetic and copies ran while one was open for 6% of the time, Pallas kernels for 0%

commit v1 on v0

--- a/solution.py
+++ b/solution.py
@@ -156,8 +156,16 @@
         + near_index[:, None]
     )
     wanted = jnp.concatenate([near_wanted, span_wanted], 0)
-    delivered = lax.all_to_all(
-        select(layout, wanted, total_blocks), "seq", split_axis=1, concat_axis=1, tiled=True
+    delivered = jnp.concatenate(
+        lax.all_to_all(
+            jnp.stack(
+                jnp.split(select(layout, wanted, total_blocks), lax.axis_size("seq"), axis=1)
+            ),
+            "seq",
+            0,
+            0,
+        ),
+        axis=1,
     )
     gathered = delivered.reshape(-1, 2 * HD)
     near_pos = (first_pos // BLOCK - window_back) * BLOCK + jnp.arange(

time: 59.8 us -> 64 us (1.070)
  local copies, waits for them, and re-layouts: 4.08 us -> 8.26 us
    unnamed x10 -> x17, local copies, waits for them, and re-layouts: 0.03 us -> 4.34 us
    gather x2 -> x1, local copies, waits for them, and re-layouts: 1.37 us -> 0.63 us  [select(): return layout[clipped % blocks_dev, clipped // blocks_dev]]
where the time goes in v1:
time: 64 us; the launch traced here: 63.6 us
  blocking collectives  30 us (47%)
  starting transfers between devices  9.23 us (14%)
  waiting for transfers between devices  8.3 us (13%)
  local copies, waits for them, and re-layouts  8.26 us (13%)
  matrix products  4.46 us (7%)
  other arithmetic  3.04 us (5%)
    all_gather x1, blocking collectives, per_device(): all_spans = lax.all_gather(span_blocks, 'seq', axis=0, tiled=True)  21 us
    all_gather x1, blocking collectives, per_device(): features = lax.all_gather(tokens, 'head', axis=1, tiled=True)  9.02 us
    all_to_all x1, waiting for transfers between devices, per_device(): lax.all_to_all(jnp.stack(jnp.split(select(layout, wanted, total_blocks),...  8.3 us
    all_to_all x1, starting transfers between devices, per_device(): lax.all_to_all(pieces, 'seq', split_axis=1, concat_axis=1, tiled=True)  5.8 us
    unnamed x17, local copies, waits for them, and re-layouts  4.34 us
    all_to_all x1, starting transfers between devices, per_device(): lax.all_to_all(jnp.stack(jnp.split(select(layout, wanted, total_blocks),...  3.43 us
    dot_general x1, matrix products, per_device(): jnp.dot(normed, value_columns, preferred_element_type=jnp.float32)  1.48 us
    dot_general x1, matrix products, per_device(): jnp.dot(normed, key_columns, preferred_element_type=jnp.float32)  1.45 us
  transfers between devices with their start and end apart: 2, of which 1 were waited for; matrix products, arithmetic and copies ran while one was open for 6% of the time, Pallas kernels for 0%

profile of v1, /device:TPU:0, one launch (start us, length us, event | category | flops | bytes accessed | tf_op | source)
XLA Modules:
  0.0 63.6 jit_solution(134616481280322877)
XLA Ops:
  0.0 0.0 copy-start
  0.1 9.0 %all_gather.6 = bf16[128,2048]{1,0:T(8,128)(2,1)S(1)} all-gather(bf16[128,512]{1,0:T(8,128)(2,1)} %param.8), channel_id=1, replica_groups=mesh['seq'=8,'head'=4] {'head'}, dimensions={1}, use_global_device_ids=true | all-gather | bytes 655360 | tf_op jit(solution)/shard_map/all_gather | solution.py:101
  9.1 0.2 fusion.4
  9.3 0.0 copy-start.3
  9.3 0.0 copy-start.4
  9.3 0.0 copy-start.2
  9.3 1.5 %convolution_convert_fusion = bf16[128,128]{0,1:T(8,128)(2,1)S(1)} fusion(bf16[2048,256]{1,0:T(8,128)(2,1)} %param.12, s32[]{:T(128)S(6)} %select_n.76, bf16[128,2048]{1,0:T(8,128)(2,1)S(1)} %all_gather.6, f32[2048]{0:T(1024)} %param.9, f32[128]{0:T(128)S(1)} %add_rsqrt_fusion), kind=kOutput, calls=%fused_computation.11 | convolution fusion | flops 68173824 | bytes 1090052 | tf_op jit(solution)/shard_map/dot_general | solution.py:123
  10.8 0.0 copy-done.1
  10.8 1.5 %convolution_bitcast_fusion = f32[128,1,128]{0,2,1:T(8,128)S(1)} fusion(bf16[2048,256]{1,0:T(8,128)(2,1)} %param.11, s32[]{:T(128)S(6)} %select_n.76, bf16[128,2048]{1,0:T(8,128)(2,1)S(1)} %all_gather.6, f32[2048]{0:T(1024)S(1)} %copy-done.1, f32[128]{0:T(128)S(1)} %add_rsqrt_fusion), kind=kOutput, calls=%fused_computation.10 | convolution fusion | flops 68157440 | bytes 1122820 | tf_op jit(solution)/shard_map/dot_general | solution.py:119
  12.3 0.2 fusion.27
  12.5 0.7 %copy.55 = bf16[128,256]{1,0:T(8,128)(2,1)} copy(bf16[128,256]{0,1:T(8,128)(2,1)S(1)} %pad_maximum_fusion) | data formatting | bytes 131072 | tf_op jit(solution)/shard_map/concatenate | solution.py:126
  13.2 5.8 %all-to-all-start = ((bf16[1,8,16,256]{3,2,0,1:T(8,128)(2,1)}), bf16[1,8,16,256]{3,2,0,1:T(8,128)(2,1)S(1)}, u32[]{:S(2)}, u32[]{:S(2)}) async-start(bf16[1,8,16,256]{3,2,0,1:T(8,128)(2,1)} %bitcast.9), calls=%async_computation | async-start | bytes 131072 | tf_op jit(solution)/shard_map/all_to_all | solution.py:133
  19.1 0.3 multiply_cosine_fusion
  19.4 0.0 copy-done.3
  19.4 0.2 reduce-window.8
  19.6 0.0 copy-done.4
  19.6 0.0 copy-done.2
  19.6 0.6 fusion.44
  20.2 0.6 add_multiply_fusion
  20.8 0.1 add.213
  20.9 0.6 fusion.32
  21.6 21.0 %all-gather = s32[8,1,2]{2,1,0:T(1,128)S(1)} all-gather(s32[1,1,2]{2,1,0:T(1,128)S(1)} %bitcast.102), channel_id=1, replica_groups=mesh['seq'=8,'head'=4] {'seq'}, dimensions={0}, use_global_device_ids=true | all-gather | bytes 72 | tf_op jit(solution)/shard_map/all_gather | solution.py:131
  42.5 0.1 copy.57
  42.7 0.1 reshape.403
  42.7 0.0 copy-done
  42.7 0.5 fusion.41
  43.2 0.1 reshape.399
  43.3 0.1 select_reduce_fusion
  43.4 0.1 compare_and_fusion
  43.6 0.1 not_and_fusion
  43.7 0.0 all-to-all-done
  43.7 0.6 gather_fusion
  44.3 0.6 fusion.25
  45.0 0.6 fusion.24
  45.6 0.6 fusion.23
  46.2 0.6 fusion.22
  46.8 0.6 fusion.21
  47.4 0.6 fusion.20
  48.0 0.6 fusion.19
  48.7 0.6 fusion.18
  49.3 3.4 %all-to-all-start.1 = ((bf16[8,5,1,16,256]{4,3,1,2,0:T(8,128)(2,1)}), bf16[8,5,1,16,256]{4,3,1,2,0:T(8,128)(2,1)S(1)}, u32[]{:S(2)}, u32[]{:S(2)}) async-start(bf16[8,5,1,16,256]{4,3,1,2,0:T(8,128)(2,1)} %fusion.18), calls=%async_computation.1 | async-start | bytes 655360 | tf_op jit(solution)/shard_map/all_to_all | solution.py:160
  52.7 0.2 fusion.43
  52.9 0.1 multiply_subtract_fusion
  53.0 8.3 %all-to-all-done.1 = bf16[8,5,1,16,256]{4,3,1,2,0:T(8,128)(2,1)S(1)} async-done(((bf16[8,5,1,16,256]{4,3,1,2,0:T(8,128)(2,1)}), bf16[8,5,1,16,256]{4,3,1,2,0:T(8,128)(2,1)S(1)}, u32[]{:S(2)}, u32[]{:S(2)}) %all-to-all-start.1) | async-done | bytes 327712 | tf_op jit(solution)/shard_map/all_to_all | solution.py:160
  61.3 0.5 fusion.45
  61.8 0.4 fusion.1
  62.3 0.5 fusion.3
  62.8 0.8 %copy.69 = bf16[128,512]{1,0:T(8,128)(2,1)} copy(bf16[128,512]{0,1:T(8,128)(2,1)S(1)} %bitcast.101) | data formatting | bytes 262144 | tf_op jit(solution)/shard_map/convert_element_type | solution.py:178
  (20 shorter events, 0.2 us)
Async XLA Ops:
  0.0 42.7 %copy-start = (bf16[2048,512]{1,0:T(8,128)(2,1)S(1)}, bf16[2048,512]{1,0:T(8,128)(2,1)}, u32[]{:S(2)}) copy-start(bf16[2048,512]{1,0:T(8,128)(2,1)} %param.10) | copy-start | bytes 6291460
  0.0 10.8 %copy-start.1 = (f32[2048]{0:T(1024)S(1)}, f32[2048]{0:T(1024)}, u32[]{:S(2)}) copy-start(f32[2048]{0:T(1024)} %param.9) | copy-start | bytes 24580
  9.3 10.1 %copy-start.3 = (s32[8]{0:T(128)S(1)}, s32[8]{0:T(128)}, u32[]{:S(2)}) copy-start(s32[8]{0:T(128)} %param.13) | copy-start | bytes 100
  9.3 10.3 %copy-start.4 = (s32[128]{0:T(128)S(1)}, s32[128]{0:T(128)}, u32[]{:S(2)}) copy-start(s32[128]{0:T(128)} %param.14) | copy-start | bytes 1540
  9.3 10.3 %copy-start.2 = (s32[1,2]{1,0:T(1,128)S(1)}, s32[1,2]{1,0:T(1,128)}, u32[]{:S(2)}) copy-start(s32[1,2]{1,0:T(1,128)} %param.15) | copy-start | bytes 28
  13.2 30.5 %all-to-all-start = ((bf16[1,8,16,256]{3,2,0,1:T(8,128)(2,1)}), bf16[1,8,16,256]{3,2,0,1:T(8,128)(2,1)S(1)}, u32[]{:S(2)}, u32[]{:S(2)}) async-start(bf16[1,8,16,256]{3,2,0,1:T(8,128)(2,1)} %bitcast.9), calls=%async_computation | async-start | bytes 131072 | tf_op jit(solution)/shard_map/all_to_all | solution.py:133
  49.3 12.0 %all-to-all-start.1 = ((bf16[8,5,1,16,256]{4,3,1,2,0:T(8,128)(2,1)}), bf16[8,5,1,16,256]{4,3,1,2,0:T(8,128)(2,1)S(1)}, u32[]{:S(2)}, u32[]{:S(2)}) async-start(bf16[8,5,1,16,256]{4,3,1,2,0:T(8,128)(2,1)} %fusion.18), calls=%async_computation.1 | async-start | bytes 655360 | tf_op jit(solution)/shard_map/all_to_all | solution.py:160
